TPU v7x, 32 devices: a whole 2x2x4 slice. The times are simulated.
32 devices in a mesh: section: 2 (over y), tensor: 4 (over z), fsdp: 4 (over x, core).
Axes of the slice: x: 2, y: 2, z: 4, core: 2. Of those that a mesh axis runs over, the one named last changes fastest.
Arguments:
- images: bfloat16 [2, 4, 729, 1152], P(None, 'fsdp'), may hold values from -6 to 6
- cotangent: bfloat16 [2, 4, 729, 1152], P(None, 'fsdp'), may hold values from -6 to 6
- qkv_weight: bfloat16 [2, 3, 1152, 1152], P('section', None, 'fsdp', 'tensor'), may hold values from -1 to 1
- qv_bias: bfloat16 [2, 2, 1152], P('section', None, 'tensor'), may hold values from -3 to 3
- out_weight: bfloat16 [2, 1152, 1152], P('section', 'tensor', 'fsdp'), may hold values from -0.75 to 0.75
- up_weight: bfloat16 [2, 1152, 4304], P('section', 'fsdp', 'tensor'), may hold values from -0.1875 to 0.1875
- up_bias: bfloat16 [2, 4304], P('section', 'tensor'), may hold values from -3 to 3
- down_weight: bfloat16 [2, 4304, 1152], P('section', 'tensor', 'fsdp'), may hold values from -0.09375 to 0.09375
- gains: bfloat16 [2, 2, 1152], P('section', None, 'fsdp'), may hold values from 0.099609375 to 1.8984375
- shifts: bfloat16 [2, 4, 1152], P('section', None, 'fsdp'), may hold values from -3 to 3
Outputs:
- section_outputs: bfloat16 [2, 2, 4, 729, 1152], P('section', None, 'fsdp')
- input_grads: bfloat16 [2, 2, 4, 729, 1152], P('section', None, 'fsdp')
- grad_qkv: float32 [2, 3, 1152, 1152], P('section', None, 'fsdp', 'tensor')
- grad_qv_bias: float32 [2, 2, 1152], P('section', None, 'tensor')
- grad_out: float32 [2, 1152, 1152], P('section', 'tensor', 'fsdp')
- grad_up: float32 [2, 1152, 4304], P('section', 'fsdp', 'tensor')
- grad_up_bias: float32 [2, 4304], P('section', 'tensor')
- grad_down: float32 [2, 4304, 1152], P('section', 'tensor', 'fsdp')
- grad_gains: float32 [2, 2, 1152], P('section', None, 'fsdp')
- grad_shifts: float32 [2, 4, 1152], P('section', None, 'fsdp')
All inputs are finite; a program needn't handle non-finite values.
Results may differ from a plain program's by a relative error of at most 0.013.
Values may be sent and summed in bfloat16 or wider, within the bound.
A program may use at most 256 MiB of HBM per device.

v0:
```python
import jax
import jax.numpy as jnp
from jax import lax
from jax.sharding import PartitionSpec as P

HD = 72
NORM_EPS = 1e-06
GELU_ROOT = 0.7978845608028654
GELU_CUBIC = 0.044715


def from_behind(value, axis, steps):
    count = lax.axis_size(axis)
    leading, last = (max(0, -steps), min(count, count - steps))
    return lax.ppermute(value, axis, [(source, source + steps) for source in range(leading, last)])


def gelu_value(value):
    return 0.5 * value * (1.0 + jnp.tanh(GELU_ROOT * (value + GELU_CUBIC * value * value * value)))


def gelu_slope(value):
    inner = jnp.tanh(GELU_ROOT * (value + GELU_CUBIC * value * value * value))
    return 0.5 * (1.0 + inner) + 0.5 * value * (1.0 - inner * inner) * GELU_ROOT * (
        1.0 + 3.0 * GELU_CUBIC * value * value
    )


def norm_forward(token_rows, gain, shift):
    mean_row = jnp.mean(token_rows, axis=-1, keepdims=True)
    centred = token_rows - mean_row
    inverse = lax.rsqrt(jnp.mean(centred * centred, axis=-1, keepdims=True) + NORM_EPS)
    normed = centred * inverse
    return (normed * gain + shift, normed, inverse)


def norm_backward(grad_normed, normed, inverse, gain):
    scaled = grad_normed * gain
    inner = (
        scaled
        - jnp.mean(scaled, axis=-1, keepdims=True)
        - normed * jnp.mean(scaled * normed, axis=-1, keepdims=True)
    )
    return (inverse * inner, jnp.sum(grad_normed * normed, axis=0), jnp.sum(grad_normed, axis=0))


def layer_forward(layer_input, weights, qv_bias, up_bias):
    qkv_weight, out_weight, up_weight, down_weight, gains, shifts = weights
    image_count, seq_len, model_width = layer_input.shape
    local_heads = qkv_weight.shape[2] // HD
    score_scale = HD ** (-0.5)
    gain_rows = gains.astype(jnp.float32)
    shift_rows = shifts.astype(jnp.float32)
    token_rows = layer_input.astype(jnp.float32).reshape(-1, model_width)
    normed_one = norm_forward(token_rows, gain_rows[0], shift_rows[0])[0].astype(jnp.bfloat16)
    projected = jnp.einsum(
        "td,cde->cte", normed_one, qkv_weight, preferred_element_type=jnp.float32
    )
    bias_rows = qv_bias.astype(jnp.float32)
    queries = (projected[0] + bias_rows[0]).astype(jnp.bfloat16)
    key_rows = projected[1].astype(jnp.bfloat16)
    values = (projected[2] + bias_rows[1]).astype(jnp.bfloat16)
    head_shape = (image_count, seq_len, local_heads, HD)
    scores = (
        jnp.einsum(
            "bqhd,bkhd->bhqk",
            queries.reshape(head_shape),
            key_rows.reshape(head_shape),
            preferred_element_type=jnp.float32,
        )
        * score_scale
    )
    row_max = jnp.max(scores, axis=-1, keepdims=True)
    exp_scores = jnp.exp(scores - row_max)
    row_total = jnp.sum(exp_scores, axis=-1, keepdims=True)
    attn_probs = (exp_scores / row_total).astype(jnp.bfloat16)
    log_total = row_max + jnp.log(row_total)
    context = jnp.einsum(
        "bhqk,bkhd->bqhd",
        attn_probs,
        values.reshape(head_shape),
        preferred_element_type=jnp.float32,
    )
    context = context.astype(jnp.bfloat16).reshape(-1, local_heads * HD)
    attn_term = jnp.dot(context, out_weight, preferred_element_type=jnp.float32)
    hidden = token_rows + lax.psum(attn_term, "tensor") + shift_rows[1]
    normed_two = norm_forward(hidden, gain_rows[1], shift_rows[2])[0].astype(jnp.bfloat16)
    pre_act = jnp.dot(normed_two, up_weight, preferred_element_type=jnp.float32) + up_bias.astype(
        jnp.float32
    )
    active = gelu_value(pre_act).astype(jnp.bfloat16)
    mlp_term = jnp.dot(active, down_weight, preferred_element_type=jnp.float32)
    output_low = (hidden + lax.psum(mlp_term, "tensor") + shift_rows[3]).astype(jnp.bfloat16)
    stored = (
        layer_input,
        normed_one,
        queries,
        key_rows,
        values,
        log_total,
        context,
        hidden,
        normed_two,
        pre_act,
        active,
    )
    return (output_low, stored)


def layer_backward(grad_output, stored, weights):
    qkv_weight, out_weight, up_weight, down_weight, gains, shifts = weights
    (
        layer_input,
        normed_one,
        queries,
        key_rows,
        values,
        log_total,
        context,
        hidden,
        normed_two,
        pre_act,
        active,
    ) = stored
    image_count, seq_len, model_width = layer_input.shape
    local_heads = qkv_weight.shape[2] // HD
    score_scale = HD ** (-0.5)
    gain_rows = gains.astype(jnp.float32)
    shift_rows = shifts.astype(jnp.float32)
    grad_mix = grad_output.astype(jnp.bfloat16)
    grad_down = jnp.einsum("tf,td->fd", active, grad_mix, preferred_element_type=jnp.float32)
    grad_active = jnp.einsum("td,fd->tf", grad_mix, down_weight, preferred_element_type=jnp.float32)
    grad_pre = (grad_active * gelu_slope(pre_act)).astype(jnp.bfloat16)
    grad_up = jnp.einsum("td,tf->df", normed_two, grad_pre, preferred_element_type=jnp.float32)
    up_bias_grad = jnp.sum(grad_pre.astype(jnp.float32), axis=0)
    two_term = jnp.einsum("tf,df->td", grad_pre, up_weight, preferred_element_type=jnp.float32)
    centred_two, inverse_two = norm_forward(hidden, gain_rows[1], shift_rows[2])[1:]
    grad_normed_two = lax.psum(two_term, "tensor")
    from_two, gain_two_grad, shift_two_grad = norm_backward(
        grad_normed_two, centred_two, inverse_two, gain_rows[1]
    )
    grad_hidden = grad_output + from_two
    grad_attn = grad_hidden.astype(jnp.bfloat16)
    attn_shift_grad = jnp.sum(grad_attn.astype(jnp.float32), axis=0)
    mix_shift_grad = jnp.sum(grad_mix.astype(jnp.float32), axis=0)
    grad_out = jnp.einsum("te,td->ed", context, grad_attn, preferred_element_type=jnp.float32)
    grad_context = jnp.einsum(
        "td,ed->te", grad_attn, out_weight, preferred_element_type=jnp.float32
    ).astype(jnp.bfloat16)
    head_shape = (image_count, seq_len, local_heads, HD)
    query_heads = queries.reshape(head_shape)
    key_heads = key_rows.reshape(head_shape)
    value_heads = values.reshape(head_shape)
    context_grads = grad_context.reshape(head_shape)
    scores = (
        jnp.einsum("bqhd,bkhd->bhqk", query_heads, key_heads, preferred_element_type=jnp.float32)
        * score_scale
    )
    probs_full = jnp.exp(scores - log_total)
    mixed = jnp.einsum(
        "bqhd,bkhd->bhqk", context_grads, value_heads, preferred_element_type=jnp.float32
    )
    row_delta = jnp.sum(mixed * probs_full, axis=-1, keepdims=True)
    grad_scores = (probs_full * (mixed - row_delta)).astype(jnp.bfloat16)
    grad_values = jnp.einsum(
        "bhqk,bqhd->bkhd",
        probs_full.astype(jnp.bfloat16),
        context_grads,
        preferred_element_type=jnp.float32,
    ).astype(jnp.bfloat16)
    grad_queries = (
        jnp.einsum("bhqk,bkhd->bqhd", grad_scores, key_heads, preferred_element_type=jnp.float32)
        * score_scale
    ).astype(jnp.bfloat16)
    grad_keys = (
        jnp.einsum("bhqk,bqhd->bkhd", grad_scores, query_heads, preferred_element_type=jnp.float32)
        * score_scale
    ).astype(jnp.bfloat16)
    flat_shape = (-1, local_heads * HD)
    grad_proj = jnp.stack(
        [
            grad_queries.reshape(flat_shape),
            grad_keys.reshape(flat_shape),
            grad_values.reshape(flat_shape),
        ]
    )
    grad_qkv = jnp.einsum("td,cte->cde", normed_one, grad_proj, preferred_element_type=jnp.float32)
    qv_bias_grad = jnp.stack(
        [
            jnp.sum(grad_proj[0].astype(jnp.float32), axis=0),
            jnp.sum(grad_proj[2].astype(jnp.float32), axis=0),
        ]
    )
    one_term = jnp.einsum("cte,cde->td", grad_proj, qkv_weight, preferred_element_type=jnp.float32)
    token_rows = layer_input.astype(jnp.float32).reshape(-1, model_width)
    grad_normed_one = lax.psum(one_term, "tensor")
    centred_one, inverse_one = norm_forward(token_rows, gain_rows[0], shift_rows[0])[1:]
    from_one, gain_one_grad, shift_one_grad = norm_backward(
        grad_normed_one, centred_one, inverse_one, gain_rows[0]
    )
    grad_low = (grad_hidden + from_one).astype(jnp.bfloat16)
    grad_gains = jnp.stack([gain_one_grad, gain_two_grad])
    grad_shifts = jnp.stack([shift_one_grad, attn_shift_grad, shift_two_grad, mix_shift_grad])
    return (
        grad_low,
        (grad_qkv, grad_out, grad_up, grad_down, grad_gains, grad_shifts),
        (qv_bias_grad, up_bias_grad),
    )


def per_device(
    images,
    cotangent,
    qkv_weight,
    qv_bias,
    out_weight,
    up_weight,
    up_bias,
    down_weight,
    gains,
    shifts,
):
    micro_count, image_count, seq_len, model_width = images.shape
    section_index = lax.axis_index("section")
    local_qv = qv_bias[0]
    local_up = up_bias[0]
    weights = (
        lax.all_gather(qkv_weight[0], "fsdp", axis=1, tiled=True),
        lax.all_gather(out_weight[0], "fsdp", axis=1, tiled=True),
        lax.all_gather(up_weight[0], "fsdp", axis=0, tiled=True),
        lax.all_gather(down_weight[0], "fsdp", axis=1, tiled=True),
        lax.all_gather(gains[0], "fsdp", axis=1, tiled=True),
        lax.all_gather(shifts[0], "fsdp", axis=1, tiled=True),
    )

    def forward_tick(carried, tick_index):
        own_input = lax.dynamic_index_in_dim(
            images, jnp.minimum(tick_index, micro_count - 1), 0, keepdims=False
        )
        layer_input = jnp.where(section_index == 0, own_input, carried)
        output_low, stored = layer_forward(layer_input, weights, local_qv, local_up)
        output_low = output_low.reshape(image_count, seq_len, model_width)
        passed = from_behind(output_low, "section", 1)
        return (passed, (output_low, stored))

    ticks = jnp.arange(micro_count + 1, dtype=jnp.int32)
    output_all, stored_all = lax.scan(forward_tick, jnp.zeros_like(images[0]), ticks)[1]
    section_outputs = lax.dynamic_slice_in_dim(output_all, section_index, micro_count, 0)
    start_sums = tuple((jnp.zeros(item.shape, jnp.float32) for item in weights))
    start_biases = (jnp.zeros(local_qv.shape, jnp.float32), jnp.zeros(local_up.shape, jnp.float32))

    def backward_tick(carry, tick_index):
        received, grad_sums, bias_totals = carry
        micro_index = micro_count - tick_index - section_index
        is_valid = (micro_index >= 0) & (micro_index < micro_count)
        safe_index = jnp.clip(micro_index, 0, micro_count - 1)
        own_grad = (
            lax.dynamic_index_in_dim(cotangent, safe_index, 0, keepdims=False)
            .astype(jnp.float32)
            .reshape(-1, model_width)
        )
        grad_output = jnp.where(section_index == 1, own_grad, received)
        stored = tuple(
            (
                lax.dynamic_index_in_dim(item, safe_index + section_index, 0, keepdims=False)
                for item in stored_all
            )
        )
        grad_low, grads, biases = layer_backward(grad_output, stored, weights)
        grads = tuple((jnp.where(is_valid, item, 0.0) for item in grads))
        biases = tuple((jnp.where(is_valid, item, 0.0) for item in biases))
        grad_low = grad_low.reshape(image_count, seq_len, model_width)
        passed = from_behind(grad_low, "section", -1).astype(jnp.float32).reshape(-1, model_width)
        grad_sums = tuple((first + second for first, second in zip(grad_sums, grads)))
        bias_totals = tuple((first + second for first, second in zip(bias_totals, biases)))
        return ((passed, grad_sums, bias_totals), grad_low)

    start_grad = jnp.zeros((image_count * seq_len, model_width), jnp.float32)
    finished, grad_all = lax.scan(backward_tick, (start_grad, start_sums, start_biases), ticks)
    grad_sums, bias_totals = (finished[1], finished[2])
    final_grads = (
        lax.psum_scatter(
            grad_sums[0].astype(jnp.bfloat16), "fsdp", scatter_dimension=1, tiled=True
        ).astype(jnp.float32),
        lax.psum_scatter(
            grad_sums[1].astype(jnp.bfloat16), "fsdp", scatter_dimension=1, tiled=True
        ).astype(jnp.float32),
        lax.psum_scatter(
            grad_sums[2].astype(jnp.bfloat16), "fsdp", scatter_dimension=0, tiled=True
        ).astype(jnp.float32),
        lax.psum_scatter(
            grad_sums[3].astype(jnp.bfloat16), "fsdp", scatter_dimension=1, tiled=True
        ).astype(jnp.float32),
        lax.psum_scatter(
            grad_sums[4].astype(jnp.bfloat16), "fsdp", scatter_dimension=1, tiled=True
        ).astype(jnp.float32),
        lax.psum_scatter(
            grad_sums[5].astype(jnp.bfloat16), "fsdp", scatter_dimension=1, tiled=True
        ).astype(jnp.float32),
    )
    final_biases = lax.psum((bias_totals[0], bias_totals[1]), "fsdp")
    gain_grads, shift_grads = (final_grads[4], final_grads[5])
    input_grads = jnp.flip(lax.dynamic_slice_in_dim(grad_all, 1 - section_index, micro_count, 0), 0)
    return (
        section_outputs[None],
        input_grads[None],
        final_grads[0][None],
        final_biases[0][None],
        final_grads[1][None],
        final_grads[2][None],
        final_biases[1][None],
        final_grads[3][None],
        gain_grads[None],
        shift_grads[None],
    )


def solution(mesh):
    return jax.shard_map(
        per_device,
        mesh=mesh,
        in_specs=(
            P(None, "fsdp", None, None),
            P(None, "fsdp", None, None),
            P("section", None, "fsdp", "tensor"),
            P("section", None, "tensor"),
            P("section", "tensor", "fsdp"),
            P("section", "fsdp", "tensor"),
            P("section", "tensor"),
            P("section", "tensor", "fsdp"),
            P("section", None, "fsdp"),
            P("section", None, "fsdp"),
        ),
        out_specs=(
            P("section", None, "fsdp", None, None),
            P("section", None, "fsdp", None, None),
            P("section", None, "fsdp", "tensor"),
            P("section", None, "tensor"),
            P("section", "tensor", "fsdp"),
            P("section", "fsdp", "tensor"),
            P("section", "tensor"),
            P("section", "tensor", "fsdp"),
            P("section", None, "fsdp"),
            P("section", None, "fsdp"),
        ),
        check_vma=False,
    )
```

profile of v0, /device:TPU:0, one launch (start us, length us, event | category | flops | bytes accessed | tf_op | source)
XLA Modules:
  0.0 2444.3 jit_solution(16826438468239682339)
XLA Ops:
  12.3 19.3 all-gather.3
  35.5 12.4 all-gather
  51.0 8.1 all-gather.1
  65.6 7.1 copy.121
  72.7 6.0 all-gather.14.cloned.1.call-done
  78.7 5.1 copy.122
  83.8 22.2 all-gather.12.cloned.1.call-done
  112.5 1034.5 %while.66 = (s32[]{:T(128)}, bf16[1,729,1152]{2,1,0:T(8,128)(2,1)}, bf16[3,1,729,1152]{3,2,1,0:T(8,128)(2,1)}, bf16[3,1,729,1152]{3,2,1,0:T(8,128)(2,1)}, bf16[3...) while((s32[]{:T(128)}, bf16[1,729,1152]{2,1,0:T(8,128)(2,1)}, ...), condition=%wide.region_9.10_spmd, body=%wide.region_0.9_spmd.sunk | while | flops 6232035840 | bytes 263704656 | solution.py:247
  145.6 130.7 %all-reduce.6.cloned.1.call-done = f32[729,1152]{1,0:T(8,128)} async-done(((f32[729,1152]{1,0:T(8,128)}), f32[729,1152]{1,0:T(8,128)}) %all-reduce.6.cloned.1.call-update) | async-done | bytes 3359248 | tf_op jit(solution)/shard_map/while/body/eval_jaxpr/psum | solution.py:86
  276.3 4.6 bitcast_dynamic-update-slice_fusion.17
  297.6 124.3 %all-reduce.8.cloned.1.call-done = f32[729,1152]{1,0:T(8,128)} async-done(((f32[729,1152]{1,0:T(8,128)}), f32[729,1152]{1,0:T(8,128)}) %all-reduce.8.cloned.1.call-update) | async-done | bytes 3359248 | tf_op jit(solution)/shard_map/while/body/eval_jaxpr/psum | solution.py:93
  426.2 4.6 collective-permute-start
  436.2 29.8 %collective-permute-done = bf16[1,729,1152]{2,1,0:T(8,128)(2,1)} collective-permute-done((bf16[1,729,1152]{2,1,0:T(8,128)(2,1)}, bf16[1,729,1152]{2,1,0:T(8,128)(2,1)}, u32[]{:S(2)}, u32[]{:S(2)}) %collective-permute-start) | collective-permute-done | bytes 1679648 | tf_op jit(solution)/shard_map/while/body/eval_jaxpr/ppermute | solution.py:15
  486.1 130.8 %all-reduce.6.cloned.1.call-done = f32[729,1152]{1,0:T(8,128)} async-done(((f32[729,1152]{1,0:T(8,128)}), f32[729,1152]{1,0:T(8,128)}) %all-reduce.6.cloned.1.call-update) | async-done | bytes 3359248 | tf_op jit(solution)/shard_map/while/body/eval_jaxpr/psum | solution.py:86
  616.9 4.7 bitcast_dynamic-update-slice_fusion.17
  638.1 124.4 %all-reduce.8.cloned.1.call-done = f32[729,1152]{1,0:T(8,128)} async-done(((f32[729,1152]{1,0:T(8,128)}), f32[729,1152]{1,0:T(8,128)}) %all-reduce.8.cloned.1.call-update) | async-done | bytes 3359248 | tf_op jit(solution)/shard_map/while/body/eval_jaxpr/psum | solution.py:93
  766.7 4.6 collective-permute-start
  776.8 29.7 %collective-permute-done = bf16[1,729,1152]{2,1,0:T(8,128)(2,1)} collective-permute-done((bf16[1,729,1152]{2,1,0:T(8,128)(2,1)}, bf16[1,729,1152]{2,1,0:T(8,128)(2,1)}, u32[]{:S(2)}, u32[]{:S(2)}) %collective-permute-start) | collective-permute-done | bytes 1679648 | tf_op jit(solution)/shard_map/while/body/eval_jaxpr/ppermute | solution.py:15
  826.6 130.8 %all-reduce.6.cloned.1.call-done = f32[729,1152]{1,0:T(8,128)} async-done(((f32[729,1152]{1,0:T(8,128)}), f32[729,1152]{1,0:T(8,128)}) %all-reduce.6.cloned.1.call-update) | async-done | bytes 3359248 | tf_op jit(solution)/shard_map/while/body/eval_jaxpr/psum | solution.py:86
  957.4 4.7 bitcast_dynamic-update-slice_fusion.17
  978.7 124.3 %all-reduce.8.cloned.1.call-done = f32[729,1152]{1,0:T(8,128)} async-done(((f32[729,1152]{1,0:T(8,128)}), f32[729,1152]{1,0:T(8,128)}) %all-reduce.8.cloned.1.call-update) | async-done | bytes 3359248 | tf_op jit(solution)/shard_map/while/body/eval_jaxpr/psum | solution.py:93
  1107.1 4.6 collective-permute-start
  1117.1 29.7 %collective-permute-done = bf16[1,729,1152]{2,1,0:T(8,128)(2,1)} collective-permute-done((bf16[1,729,1152]{2,1,0:T(8,128)(2,1)}, bf16[1,729,1152]{2,1,0:T(8,128)(2,1)}, u32[]{:S(2)}, u32[]{:S(2)}) %collective-permute-start) | collective-permute-done | bytes 1679648 | tf_op jit(solution)/shard_map/while/body/eval_jaxpr/ppermute | solution.py:15
  1149.9 1104.1 %while.67 = (s32[]{:T(128)}, f32[729,1152]{1,0:T(8,128)S(1)}, f32[3,1152,288]{1,2,0:T(8,128)}, f32[288,1152]{1,0:T(8,128)}, f32[1152,1076]{0,1:T(8,128)}, /*inde...) while((s32[]{:T(128)}, f32[729,1152]{1,0:T(8,128)S(1)}, ...), condition=%wide.region_31.32_spmd.clone, body=%wide.region_10.31_spmd.clone.sunk | while | flops 12738733056 | bytes 490833920 | solution.py:279
  1175.0 6.1 convert_reduce_fusion.16
  1195.7 4.9 fusion.210
  1200.5 115.7 %all-reduce.10.cloned.1.call-done = f32[729,1152]{1,0:T(8,128)} async-done(((f32[729,1152]{1,0:T(8,128)}), f32[729,1152]{1,0:T(8,128)}) %all-reduce.10.cloned.1.call-update) | async-done | bytes 3359248 | tf_op jit(solution)/shard_map/while/body/eval_jaxpr/psum | solution.py:138
  1316.2 4.5 multiply_reduce_fusion.16
  1327.0 4.7 multiply_reduce_fusion.17
  1331.7 10.2 multiply_convert_fusion.2
  1347.2 5.5 convert_reduce_fusion.18
  1361.9 6.2 fusion.215
  1368.2 5.2 fusion.216
  1378.7 106.2 %all-reduce.12.cloned.1.call-done = f32[729,1152]{1,0:T(8,128)} async-done(((f32[729,1152]{1,0:T(8,128)}), f32[729,1152]{1,0:T(8,128)}) %all-reduce.12.cloned.1.call-update) | async-done | bytes 3359248 | tf_op jit(solution)/shard_map/while/body/eval_jaxpr/psum | solution.py:196
  1498.5 34.7 %collective-permute-done.1 = bf16[1,729,1152]{2,1,0:T(8,128)(2,1)S(1)} collective-permute-done((bf16[1,729,1152]{2,1,0:T(8,128)(2,1)S(1)}, bf16[1,729,1152]{2,1,0:T(8,128)(2,1)S(1)}, u32[]{:S(2)}, u32[]{:S(2)}) %collective-permute-start.1) | collective-permute-done | bytes 1679648 | tf_op jit(solution)/shard_map/while/body/eval_jaxpr/ppermute | solution.py:15
  1537.1 6.1 convert_reduce_fusion.16
  1557.9 4.9 fusion.210
  1562.8 113.6 %all-reduce.10.cloned.1.call-done = f32[729,1152]{1,0:T(8,128)} async-done(((f32[729,1152]{1,0:T(8,128)}), f32[729,1152]{1,0:T(8,128)}) %all-reduce.10.cloned.1.call-update) | async-done | bytes 3359248 | tf_op jit(solution)/shard_map/while/body/eval_jaxpr/psum | solution.py:138
  1676.4 4.5 multiply_reduce_fusion.16
  1687.2 4.7 multiply_reduce_fusion.17
  1691.9 10.2 multiply_convert_fusion.2
  1707.4 5.5 convert_reduce_fusion.18
  1722.2 7.7 fusion.215
  1729.9 5.2 fusion.216
  1740.9 104.2 %all-reduce.12.cloned.1.call-done = f32[729,1152]{1,0:T(8,128)} async-done(((f32[729,1152]{1,0:T(8,128)}), f32[729,1152]{1,0:T(8,128)}) %all-reduce.12.cloned.1.call-update) | async-done | bytes 3359248 | tf_op jit(solution)/shard_map/while/body/eval_jaxpr/psum | solution.py:196
  1858.7 34.7 %collective-permute-done.1 = bf16[1,729,1152]{2,1,0:T(8,128)(2,1)S(1)} collective-permute-done((bf16[1,729,1152]{2,1,0:T(8,128)(2,1)S(1)}, bf16[1,729,1152]{2,1,0:T(8,128)(2,1)S(1)}, u32[]{:S(2)}, u32[]{:S(2)}) %collective-permute-start.1) | collective-permute-done | bytes 1679648 | tf_op jit(solution)/shard_map/while/body/eval_jaxpr/ppermute | solution.py:15
  1897.3 6.1 convert_reduce_fusion.16
  1918.1 4.9 fusion.210
  1922.9 113.6 %all-reduce.10.cloned.1.call-done = f32[729,1152]{1,0:T(8,128)} async-done(((f32[729,1152]{1,0:T(8,128)}), f32[729,1152]{1,0:T(8,128)}) %all-reduce.10.cloned.1.call-update) | async-done | bytes 3359248 | tf_op jit(solution)/shard_map/while/body/eval_jaxpr/psum | solution.py:138
  2047.2 4.7 multiply_reduce_fusion.17
  2051.8 10.2 multiply_convert_fusion.2
  2067.4 5.5 convert_reduce_fusion.18
  2082.2 7.7 fusion.215
  2089.9 5.2 fusion.216
  2100.9 104.2 %all-reduce.12.cloned.1.call-done = f32[729,1152]{1,0:T(8,128)} async-done(((f32[729,1152]{1,0:T(8,128)}), f32[729,1152]{1,0:T(8,128)}) %all-reduce.12.cloned.1.call-update) | async-done | bytes 3359248 | tf_op jit(solution)/shard_map/while/body/eval_jaxpr/psum | solution.py:196
  2218.7 34.7 %collective-permute-done.1 = bf16[1,729,1152]{2,1,0:T(8,128)(2,1)S(1)} collective-permute-done((bf16[1,729,1152]{2,1,0:T(8,128)(2,1)S(1)}, bf16[1,729,1152]{2,1,0:T(8,128)(2,1)S(1)}, u32[]{:S(2)}, u32[]{:S(2)}) %collective-permute-start.1) | collective-permute-done | bytes 1679648 | tf_op jit(solution)/shard_map/while/body/eval_jaxpr/ppermute | solution.py:15
  2262.4 6.0 copy.137
  2285.4 6.0 copy.129
  2291.3 5.2 constant_dynamic-slice_fusion.3
  2296.5 31.6 %rev.4 = bf16[2,1,729,1152]{3,0,2,1:T(2,128)(2,1)} reverse(bf16[2,1,729,1152]{3,0,2,1:T(2,128)(2,1)} %constant_dynamic-slice_fusion.3), dimensions={0} | reverse | bytes 6718464 | tf_op jit(solution)/shard_map/jit(_flip)/rev | solution.py:303
  2334.8 6.5 all-reduce
  2346.4 13.1 reduce-scatter.19.cloned.1.call-done
  2364.7 32.0 %reduce-scatter.23.cloned.1.call-done = bf16[288,1076]{1,0:T(8,128)(2,1)} async-done(((bf16[1152,1076]{1,0:T(8,128)(2,1)}), bf16[288,1076]{1,0:T(8,128)(2,1)}) %reduce-scatter.23.cloned.1.call-update) | async-done | bytes 619792
  2399.9 34.1 %reduce-scatter.25.cloned.1.call-done = bf16[288,1076]{1,0:T(8,128)(2,1)} async-done(((bf16[1152,1076]{1,0:T(8,128)(2,1)}), bf16[288,1076]{1,0:T(8,128)(2,1)}) %reduce-scatter.25.cloned.1.call-update) | async-done | bytes 619792
  (758 shorter events, 388.6 us)
Async XLA Ops:
  7.2 58.4 %all-gather.10.cloned.1.call-start = ((), (), s32[]{:S(2)}) async-start(), calls=%async_computation.6 | async-start | bytes 4423680 | tf_op jit(solution)/shard_map/all_gather | solution.py:228
  9.8 25.6 %copy-start.65 = (bf16[1,2,288]{2,1,0:T(2,128)(2,1)S(1)}, bf16[1,2,288]{2,1,0:T(2,128)(2,1)}, u32[]{:S(2)}) copy-start(bf16[1,2,288]{2,1,0:T(2,128)(2,1)} %param.22) | copy-start | bytes 3460
  9.8 68.9 %all-gather.14.cloned.1.call-start = ((), (), s32[]{:S(2)}) async-start(), calls=%async_computation.8 | async-start | bytes 3317760 | tf_op jit(solution)/shard_map/all_gather | solution.py:231
  10.5 95.4 %all-gather.12.cloned.1.call-start = ((), (), s32[]{:S(2)}) async-start(), calls=%async_computation.7 | async-start | bytes 3317760 | tf_op jit(solution)/shard_map/all_gather | solution.py:230
  125.5 150.8 %all-reduce.6.cloned.1.call-start = ((), (), s32[]{:S(2)}) async-start(), calls=%async_computation.15 | async-start | bytes 6782976 | tf_op jit(solution)/shard_map/while/body/eval_jaxpr/psum | solution.py:86
  142.6 133.7 %copy-start.42 = (f32[1152]{0:T(1024)S(1)}, f32[1152]{0:T(1024)}, u32[]{:S(2)}) copy-start(f32[1152]{0:T(1024)} %get-tuple-element.1532) | copy-start | bytes 13828 | tf_op jit(solution)/shard_map/while
  145.5 276.4 %all-reduce.8.cloned.1.call-start = ((), (), s32[]{:S(2)}) async-start(), calls=%async_computation.16 | async-start | bytes 6782976 | tf_op jit(solution)/shard_map/while/body/eval_jaxpr/psum | solution.py:93
  293.6 128.4 %copy-start.43 = (f32[1152]{0:T(1024)S(1)}, f32[1152]{0:T(1024)}, u32[]{:S(2)}) copy-start(f32[1152]{0:T(1024)} %get-tuple-element.1531) | copy-start | bytes 13828 | tf_op jit(solution)/shard_map/while
  421.9 8.8 copy-start.21
  426.2 39.8 %collective-permute-start = (bf16[1,729,1152]{2,1,0:T(8,128)(2,1)}, bf16[1,729,1152]{2,1,0:T(8,128)(2,1)}, u32[]{:S(2)}, u32[]{:S(2)}) collective-permute-start(bf16[1,729,1152]{2,1,0:T(8,128)(2,1)} %bitcast.319), channel_id=1, source_target_pairs={{0,16},{1,17},{2,18},{3,19},{4,20},{5,21},{6,22},{7,23},{8,24},{9,... | collective-permute-start | bytes 5038856 | tf_op jit(solution)/shard_map/while/body/eval_jaxpr/ppermute | solution.py:15
  433.9 32.0 %copy-start.29 = (bf16[2,1,729,1152]{3,2,1,0:T(8,128)(2,1)S(1)}, bf16[2,1,729,1152]{3,2,1,0:T(8,128)(2,1)}, u32[]{:S(2)}) copy-start(bf16[2,1,729,1152]{3,2,1,0:T(8,128)(2,1)} %copy-done.28) | copy-start | bytes 10077700 | tf_op jit(solution)/shard_map/while
  433.9 32.0 %copy-start.46 = (bf16[2,1152]{1,0:T(2,128)(2,1)S(1)}, bf16[2,1152]{1,0:T(2,128)(2,1)}, u32[]{:S(2)}) copy-start(bf16[2,1152]{1,0:T(2,128)(2,1)} %copy-done.45) | copy-start | bytes 13828 | tf_op jit(solution)/shard_map/while
  433.9 32.0 %copy-start.51 = (bf16[4,1152]{1,0:T(4,128)(2,1)S(1)}, bf16[4,1152]{1,0:T(4,128)(2,1)}, u32[]{:S(2)}) copy-start(bf16[4,1152]{1,0:T(4,128)(2,1)} %copy-done.50) | copy-start | bytes 27652 | tf_op jit(solution)/shard_map/while
  433.9 32.0 %copy-start.61 = (bf16[1,2,288]{2,1,0:T(2,128)(2,1)S(1)}, bf16[1,2,288]{2,1,0:T(2,128)(2,1)}, u32[]{:S(2)}) copy-start(bf16[1,2,288]{2,1,0:T(2,128)(2,1)} %get-tuple-element.1899) | copy-start | bytes 3460 | tf_op jit(solution)/shard_map/while
  433.9 32.0 %copy-start.69 = (s32[3]{0:T(128)S(1)}, s32[3]{0:T(128)}, u32[]{:S(2)}) copy-start(s32[3]{0:T(128)} %copy-done.68) | copy-start | bytes 40 | tf_op jit(solution)/shard_map/while
  466.0 150.8 %all-reduce.6.cloned.1.call-start = ((), (), s32[]{:S(2)}) async-start(), calls=%async_computation.15 | async-start | bytes 6782976 | tf_op jit(solution)/shard_map/while/body/eval_jaxpr/psum | solution.py:86
  483.1 133.8 %copy-start.42 = (f32[1152]{0:T(1024)S(1)}, f32[1152]{0:T(1024)}, u32[]{:S(2)}) copy-start(f32[1152]{0:T(1024)} %get-tuple-element.1532) | copy-start | bytes 13828 | tf_op jit(solution)/shard_map/while
  486.0 276.4 %all-reduce.8.cloned.1.call-start = ((), (), s32[]{:S(2)}) async-start(), calls=%async_computation.16 | async-start | bytes 6782976 | tf_op jit(solution)/shard_map/while/body/eval_jaxpr/psum | solution.py:93
  634.1 128.4 %copy-start.43 = (f32[1152]{0:T(1024)S(1)}, f32[1152]{0:T(1024)}, u32[]{:S(2)}) copy-start(f32[1152]{0:T(1024)} %get-tuple-element.1531) | copy-start | bytes 13828 | tf_op jit(solution)/shard_map/while
  762.4 8.8 copy-start.21
  766.7 39.8 %collective-permute-start = (bf16[1,729,1152]{2,1,0:T(8,128)(2,1)}, bf16[1,729,1152]{2,1,0:T(8,128)(2,1)}, u32[]{:S(2)}, u32[]{:S(2)}) collective-permute-start(bf16[1,729,1152]{2,1,0:T(8,128)(2,1)} %bitcast.319), channel_id=1, source_target_pairs={{0,16},{1,17},{2,18},{3,19},{4,20},{5,21},{6,22},{7,23},{8,24},{9,... | collective-permute-start | bytes 5038856 | tf_op jit(solution)/shard_map/while/body/eval_jaxpr/ppermute | solution.py:15
  774.5 32.0 %copy-start.29 = (bf16[2,1,729,1152]{3,2,1,0:T(8,128)(2,1)S(1)}, bf16[2,1,729,1152]{3,2,1,0:T(8,128)(2,1)}, u32[]{:S(2)}) copy-start(bf16[2,1,729,1152]{3,2,1,0:T(8,128)(2,1)} %copy-done.28) | copy-start | bytes 10077700 | tf_op jit(solution)/shard_map/while
  774.5 32.0 %copy-start.46 = (bf16[2,1152]{1,0:T(2,128)(2,1)S(1)}, bf16[2,1152]{1,0:T(2,128)(2,1)}, u32[]{:S(2)}) copy-start(bf16[2,1152]{1,0:T(2,128)(2,1)} %copy-done.45) | copy-start | bytes 13828 | tf_op jit(solution)/shard_map/while
  774.5 32.0 %copy-start.51 = (bf16[4,1152]{1,0:T(4,128)(2,1)S(1)}, bf16[4,1152]{1,0:T(4,128)(2,1)}, u32[]{:S(2)}) copy-start(bf16[4,1152]{1,0:T(4,128)(2,1)} %copy-done.50) | copy-start | bytes 27652 | tf_op jit(solution)/shard_map/while
  774.5 32.0 %copy-start.61 = (bf16[1,2,288]{2,1,0:T(2,128)(2,1)S(1)}, bf16[1,2,288]{2,1,0:T(2,128)(2,1)}, u32[]{:S(2)}) copy-start(bf16[1,2,288]{2,1,0:T(2,128)(2,1)} %get-tuple-element.1899) | copy-start | bytes 3460 | tf_op jit(solution)/shard_map/while
  774.5 32.0 %copy-start.69 = (s32[3]{0:T(128)S(1)}, s32[3]{0:T(128)}, u32[]{:S(2)}) copy-start(s32[3]{0:T(128)} %copy-done.68) | copy-start | bytes 40 | tf_op jit(solution)/shard_map/while
  806.5 150.8 %all-reduce.6.cloned.1.call-start = ((), (), s32[]{:S(2)}) async-start(), calls=%async_computation.15 | async-start | bytes 6782976 | tf_op jit(solution)/shard_map/while/body/eval_jaxpr/psum | solution.py:86
  823.6 133.8 %copy-start.42 = (f32[1152]{0:T(1024)S(1)}, f32[1152]{0:T(1024)}, u32[]{:S(2)}) copy-start(f32[1152]{0:T(1024)} %get-tuple-element.1532) | copy-start | bytes 13828 | tf_op jit(solution)/shard_map/while
  826.5 276.4 %all-reduce.8.cloned.1.call-start = ((), (), s32[]{:S(2)}) async-start(), calls=%async_computation.16 | async-start | bytes 6782976 | tf_op jit(solution)/shard_map/while/body/eval_jaxpr/psum | solution.py:93
  974.6 128.4 %copy-start.43 = (f32[1152]{0:T(1024)S(1)}, f32[1152]{0:T(1024)}, u32[]{:S(2)}) copy-start(f32[1152]{0:T(1024)} %get-tuple-element.1531) | copy-start | bytes 13828 | tf_op jit(solution)/shard_map/while
  1103.0 8.7 copy-start.21
  1107.1 39.8 %collective-permute-start = (bf16[1,729,1152]{2,1,0:T(8,128)(2,1)}, bf16[1,729,1152]{2,1,0:T(8,128)(2,1)}, u32[]{:S(2)}, u32[]{:S(2)}) collective-permute-start(bf16[1,729,1152]{2,1,0:T(8,128)(2,1)} %bitcast.319), channel_id=1, source_target_pairs={{0,16},{1,17},{2,18},{3,19},{4,20},{5,21},{6,22},{7,23},{8,24},{9,... | collective-permute-start | bytes 5038856 | tf_op jit(solution)/shard_map/while/body/eval_jaxpr/ppermute | solution.py:15
  1114.9 32.0 %copy-start.29 = (bf16[2,1,729,1152]{3,2,1,0:T(8,128)(2,1)S(1)}, bf16[2,1,729,1152]{3,2,1,0:T(8,128)(2,1)}, u32[]{:S(2)}) copy-start(bf16[2,1,729,1152]{3,2,1,0:T(8,128)(2,1)} %copy-done.28) | copy-start | bytes 10077700 | tf_op jit(solution)/shard_map/while
  1114.9 32.0 %copy-start.46 = (bf16[2,1152]{1,0:T(2,128)(2,1)S(1)}, bf16[2,1152]{1,0:T(2,128)(2,1)}, u32[]{:S(2)}) copy-start(bf16[2,1152]{1,0:T(2,128)(2,1)} %copy-done.45) | copy-start | bytes 13828 | tf_op jit(solution)/shard_map/while
  1114.9 32.0 %copy-start.51 = (bf16[4,1152]{1,0:T(4,128)(2,1)S(1)}, bf16[4,1152]{1,0:T(4,128)(2,1)}, u32[]{:S(2)}) copy-start(bf16[4,1152]{1,0:T(4,128)(2,1)} %copy-done.50) | copy-start | bytes 27652 | tf_op jit(solution)/shard_map/while
  1114.9 32.0 %copy-start.61 = (bf16[1,2,288]{2,1,0:T(2,128)(2,1)S(1)}, bf16[1,2,288]{2,1,0:T(2,128)(2,1)}, u32[]{:S(2)}) copy-start(bf16[1,2,288]{2,1,0:T(2,128)(2,1)} %get-tuple-element.1899) | copy-start | bytes 3460 | tf_op jit(solution)/shard_map/while
  1114.9 32.0 %copy-start.69 = (s32[3]{0:T(128)S(1)}, s32[3]{0:T(128)}, u32[]{:S(2)}) copy-start(s32[3]{0:T(128)} %copy-done.68) | copy-start | bytes 40 | tf_op jit(solution)/shard_map/while
  1171.3 144.9 %all-reduce.10.cloned.1.call-start = ((), (), s32[]{:S(2)}) async-start(), calls=%async_computation.17 | async-start | bytes 6782976 | tf_op jit(solution)/shard_map/while/body/eval_jaxpr/psum | solution.py:138
  1175.0 7.4 copy-start.67
  1186.8 298.1 %all-reduce.12.cloned.1.call-start = ((), (), s32[]{:S(2)}) async-start(), calls=%async_computation.18 | async-start | bytes 6782976 | tf_op jit(solution)/shard_map/while/body/eval_jaxpr/psum | solution.py:196
  1357.5 10.6 slice-start.3
  1492.7 40.5 %collective-permute-start.1 = (bf16[1,729,1152]{2,1,0:T(8,128)(2,1)S(1)}, bf16[1,729,1152]{2,1,0:T(8,128)(2,1)S(1)}, u32[]{:S(2)}, u32[]{:S(2)}) collective-permute-start(bf16[1,729,1152]{2,1,0:T(8,128)(2,1)S(1)} %bitcast.382), channel_id=1, source_target_pairs={{16,0},{17,1},{18,2},{19,3},{20,4},{21,5},{22,6},{23,7},{24,8},{25... | collective-permute-start | bytes 5038856 | tf_op jit(solution)/shard_map/while/body/eval_jaxpr/ppermute | solution.py:15
  1498.4 35.0 %copy-start.33 = (f32[3,1152,288]{1,2,0:T(8,128)}, f32[3,1152,288]{1,2,0:T(8,128)S(1)}, u32[]{:S(2)}) copy-start(f32[3,1152,288]{1,2,0:T(8,128)S(1)} %bitcast_add_fusion.2) | copy-start | bytes 11943940 | tf_op jit(solution)/shard_map/while
  1533.4 143.0 %all-reduce.10.cloned.1.call-start = ((), (), s32[]{:S(2)}) async-start(), calls=%async_computation.17 | async-start | bytes 6782976 | tf_op jit(solution)/shard_map/while/body/eval_jaxpr/psum | solution.py:138
  1548.9 296.2 %all-reduce.12.cloned.1.call-start = ((), (), s32[]{:S(2)}) async-start(), calls=%async_computation.18 | async-start | bytes 6782976 | tf_op jit(solution)/shard_map/while/body/eval_jaxpr/psum | solution.py:196
  1717.7 12.1 slice-start.3
  1722.1 7.7 copy-start.27
  1722.1 7.7 slice-start.4
  1852.9 40.5 %collective-permute-start.1 = (bf16[1,729,1152]{2,1,0:T(8,128)(2,1)S(1)}, bf16[1,729,1152]{2,1,0:T(8,128)(2,1)S(1)}, u32[]{:S(2)}, u32[]{:S(2)}) collective-permute-start(bf16[1,729,1152]{2,1,0:T(8,128)(2,1)S(1)} %bitcast.382), channel_id=1, source_target_pairs={{16,0},{17,1},{18,2},{19,3},{20,4},{21,5},{22,6},{23,7},{24,8},{25... | collective-permute-start | bytes 5038856 | tf_op jit(solution)/shard_map/while/body/eval_jaxpr/ppermute | solution.py:15
  1858.6 35.0 %copy-start.33 = (f32[3,1152,288]{1,2,0:T(8,128)}, f32[3,1152,288]{1,2,0:T(8,128)S(1)}, u32[]{:S(2)}) copy-start(f32[3,1152,288]{1,2,0:T(8,128)S(1)} %bitcast_add_fusion.2) | copy-start | bytes 11943940 | tf_op jit(solution)/shard_map/while
  1893.6 143.0 %all-reduce.10.cloned.1.call-start = ((), (), s32[]{:S(2)}) async-start(), calls=%async_computation.17 | async-start | bytes 6782976 | tf_op jit(solution)/shard_map/while/body/eval_jaxpr/psum | solution.py:138
  1897.3 7.4 copy-start.67
  1909.1 296.0 %all-reduce.12.cloned.1.call-start = ((), (), s32[]{:S(2)}) async-start(), calls=%async_computation.18 | async-start | bytes 6782976 | tf_op jit(solution)/shard_map/while/body/eval_jaxpr/psum | solution.py:196
  2077.7 12.1 slice-start.3
  2082.1 7.7 copy-start.27
  2082.1 7.7 slice-start.4
  2212.9 40.5 %collective-permute-start.1 = (bf16[1,729,1152]{2,1,0:T(8,128)(2,1)S(1)}, bf16[1,729,1152]{2,1,0:T(8,128)(2,1)S(1)}, u32[]{:S(2)}, u32[]{:S(2)}) collective-permute-start(bf16[1,729,1152]{2,1,0:T(8,128)(2,1)S(1)} %bitcast.382), channel_id=1, source_target_pairs={{16,0},{17,1},{18,2},{19,3},{20,4},{21,5},{22,6},{23,7},{24,8},{25... | collective-permute-start | bytes 5038856 | tf_op jit(solution)/shard_map/while/body/eval_jaxpr/ppermute | solution.py:15
  2218.6 35.0 %copy-start.33 = (f32[3,1152,288]{1,2,0:T(8,128)}, f32[3,1152,288]{1,2,0:T(8,128)S(1)}, u32[]{:S(2)}) copy-start(f32[3,1152,288]{1,2,0:T(8,128)S(1)} %bitcast_add_fusion.2) | copy-start | bytes 11943940 | tf_op jit(solution)/shard_map/while
  2254.0 87.3 %reduce-scatter.27.cloned.1.call-start = ((), (), s32[]{:S(2)}) async-start(), calls=%async_computation.13 | async-start | bytes 368640
  2255.0 87.9 %reduce-scatter.29.cloned.1.call-start = ((), (), s32[]{:S(2)}) async-start(), calls=%async_computation.14 | async-start | bytes 368640
  2256.0 88.4 %reduce-scatter.21.cloned.1.call-start = ((), (), s32[]{:S(2)}) async-start(), calls=%async_computation.10 | async-start | bytes 1105920
  2258.7 100.9 %reduce-scatter.19.cloned.1.call-start = ((), (), s32[]{:S(2)}) async-start(), calls=%async_computation.9 | async-start | bytes 2580480
  2272.6 124.2 %reduce-scatter.23.cloned.1.call-start = ((), (), s32[]{:S(2)}) async-start(), calls=%async_computation.11 | async-start | bytes 3317760
  2278.6 155.4 %reduce-scatter.25.cloned.1.call-start = ((), (), s32[]{:S(2)}) async-start(), calls=%async_computation.12 | async-start | bytes 3317760
  (170 other events, 567.4 us)
Sparse Core Ops, SparseCore 0:
  10.1 40.3 all-gather.9
  52.1 26.5 all-gather.13
  80.2 25.7 all-gather.11
  145.7 130.6 all-reduce.5
  293.7 128.1 all-reduce.7
  486.1 130.6 all-reduce.5
  634.2 128.1 all-reduce.7
  826.7 130.6 all-reduce.5
  974.8 128.1 all-reduce.7
  1186.9 129.2 all-reduce.9
  1357.6 127.2 all-reduce.11
  1549.1 127.3 all-reduce.9
  1717.8 127.2 all-reduce.11
  1909.2 127.3 all-reduce.9
  2077.8 127.2 all-reduce.11
  2257.6 18.3 reduce-scatter.26
  2278.9 20.2 reduce-scatter.28
  2302.2 23.7 reduce-scatter.20
  2328.6 30.9 reduce-scatter.18
  2362.0 34.7 reduce-scatter.22
  2399.3 34.7 reduce-scatter.24
where the time goes:
time: 2450 us; the launch traced here: 2440 us
  waiting for transfers between devices  1730 us (71%)
  matrix products  218 us (9%)
  other arithmetic  196 us (8%)
  local copies, waits for them, and re-layouts  184 us (8%)
  blocking collectives  46.4 us (2%)
  loops' own time  41.8 us (2%)
    psum x3, waiting for transfers between devices, layer_forward(): hidden = token_rows + lax.psum(attn_term, 'tensor') + shift_rows[1]  392 us
    psum x3, waiting for transfers between devices, layer_forward(): lax.psum(mlp_term, 'tensor')  373 us
    psum x3, waiting for transfers between devices, layer_backward(): grad_normed_two = lax.psum(two_term, 'tensor')  343 us
    psum x3, waiting for transfers between devices, layer_backward(): grad_normed_one = lax.psum(one_term, 'tensor')  315 us
    ppermute x6, waiting for transfers between devices, from_behind(): lax.ppermute(value, axis, [(source, source + steps) for source in range(l...  193 us
    unnamed x15, waiting for transfers between devices  80.8 us
    dynamic_update_slice x27, other arithmetic, per_device(): lax.scan(forward_tick, jnp.zeros_like(images[0]), ticks)[1]  69.8 us
  transfers between devices with their start and end apart: 27, of which 23 were waited for; matrix products, arithmetic and copies ran while one was open for 11% of the time, Pallas kernels for 0%

commit v1 on v0

--- a/solution.py
+++ b/solution.py
@@ -135,7 +135,7 @@
     up_bias_grad = jnp.sum(grad_pre.astype(jnp.float32), axis=0)
     two_term = jnp.einsum("tf,df->td", grad_pre, up_weight, preferred_element_type=jnp.float32)
     centred_two, inverse_two = norm_forward(hidden, gain_rows[1], shift_rows[2])[1:]
-    grad_normed_two = lax.psum(two_term, "tensor")
+    grad_normed_two = jnp.sum(lax.all_gather(two_term, "tensor"), axis=0)
     from_two, gain_two_grad, shift_two_grad = norm_backward(
         grad_normed_two, centred_two, inverse_two, gain_rows[1]
     )

time: 2450 us -> 2790 us (1.14)
  waiting for transfers between devices: 1730 us -> 2030 us
    all_gather x0 -> x3, waiting for transfers between devices: none -> 655 us  [layer_backward(): grad_normed_two = jnp.sum(lax.all_gather(two_term, 'tensor'), axis=0)]
    psum x3 -> x0, waiting for transfers between devices: 343 us -> none  [layer_backward(): grad_normed_two = lax.psum(two_term, 'tensor')]
  transfers between devices with their start and end apart: 27 -> 27, of which waited for: 23 -> 23; matrix products, arithmetic and copies ran while one was open for 11% -> 10% of each run, Pallas kernels for 0% -> 0%
where the time goes in v1:
time: 2790 us; the launch traced here: 2780 us
  waiting for transfers between devices  2030 us (73%)
  matrix products  220 us (8%)
  other arithmetic  216 us (8%)
  local copies, waits for them, and re-layouts  184 us (7%)
  blocking collectives  46.4 us (2%)
  loops' own time  45.3 us (2%)
    all_gather x3, waiting for transfers between devices, layer_backward(): grad_normed_two = jnp.sum(lax.all_gather(two_term, 'tensor'), axis=0)  655 us
    psum x3, waiting for transfers between devices, layer_forward(): hidden = token_rows + lax.psum(attn_term, 'tensor') + shift_rows[1]  392 us
    psum x3, waiting for transfers between devices, layer_forward(): lax.psum(mlp_term, 'tensor')  373 us
    psum x3, waiting for transfers between devices, layer_backward(): grad_normed_one = lax.psum(one_term, 'tensor')  311 us
    ppermute x6, waiting for transfers between devices, from_behind(): lax.ppermute(value, axis, [(source, source + steps) for source in range(l...  193 us
    unnamed x15, waiting for transfers between devices  80.7 us
    dynamic_update_slice x27, other arithmetic, per_device(): lax.scan(forward_tick, jnp.zeros_like(images[0]), ticks)[1]  69.7 us
  transfers between devices with their start and end apart: 27, of which 23 were waited for; matrix products, arithmetic and copies ran while one was open for 10% of the time, Pallas kernels for 0%

profile of v1, /device:TPU:0, one launch (start us, length us, event | category | flops | bytes accessed | tf_op | source)
XLA Modules:
  0.0 2777.9 jit_solution(7784001579431533880)
XLA Ops:
  12.3 19.3 all-gather.4
  35.6 12.4 all-gather.1
  51.0 8.2 all-gather.2
  65.6 7.1 copy.121
  72.7 5.9 all-gather.20.cloned.1.call-done
  78.7 5.1 copy.122
  83.8 22.2 all-gather.18.cloned.1.call-done
  112.4 1034.2 %while.66 = (s32[]{:T(128)}, bf16[1,729,1152]{2,1,0:T(8,128)(2,1)}, bf16[3,1,729,1152]{3,2,1,0:T(8,128)(2,1)}, bf16[3,1,729,1152]{3,2,1,0:T(8,128)(2,1)}, bf16[3...) while((s32[]{:T(128)}, bf16[1,729,1152]{2,1,0:T(8,128)(2,1)}, ...), condition=%wide.region_9.10_spmd, body=%wide.region_0.9_spmd.sunk | while | flops 6232035840 | bytes 263704656 | solution.py:247
  145.5 130.7 %all-reduce.5.cloned.1.call-done = f32[729,1152]{1,0:T(8,128)} async-done(((f32[729,1152]{1,0:T(8,128)}), f32[729,1152]{1,0:T(8,128)}) %all-reduce.5.cloned.1.call-update) | async-done | bytes 3359248 | tf_op jit(solution)/shard_map/while/body/eval_jaxpr/psum | solution.py:86
  276.3 4.6 bitcast_dynamic-update-slice_fusion.17
  297.5 124.3 %all-reduce.7.cloned.1.call-done = f32[729,1152]{1,0:T(8,128)} async-done(((f32[729,1152]{1,0:T(8,128)}), f32[729,1152]{1,0:T(8,128)}) %all-reduce.7.cloned.1.call-update) | async-done | bytes 3359248 | tf_op jit(solution)/shard_map/while/body/eval_jaxpr/psum | solution.py:93
  436.1 29.7 %collective-permute-done = bf16[1,729,1152]{2,1,0:T(8,128)(2,1)} collective-permute-done((bf16[1,729,1152]{2,1,0:T(8,128)(2,1)}, bf16[1,729,1152]{2,1,0:T(8,128)(2,1)}, u32[]{:S(2)}, u32[]{:S(2)}) %collective-permute-start) | collective-permute-done | bytes 1679648 | tf_op jit(solution)/shard_map/while/body/eval_jaxpr/ppermute | solution.py:15
  486.0 130.8 %all-reduce.5.cloned.1.call-done = f32[729,1152]{1,0:T(8,128)} async-done(((f32[729,1152]{1,0:T(8,128)}), f32[729,1152]{1,0:T(8,128)}) %all-reduce.5.cloned.1.call-update) | async-done | bytes 3359248 | tf_op jit(solution)/shard_map/while/body/eval_jaxpr/psum | solution.py:86
  616.7 4.6 bitcast_dynamic-update-slice_fusion.17
  638.0 124.3 %all-reduce.7.cloned.1.call-done = f32[729,1152]{1,0:T(8,128)} async-done(((f32[729,1152]{1,0:T(8,128)}), f32[729,1152]{1,0:T(8,128)}) %all-reduce.7.cloned.1.call-update) | async-done | bytes 3359248 | tf_op jit(solution)/shard_map/while/body/eval_jaxpr/psum | solution.py:93
  776.6 29.7 %collective-permute-done = bf16[1,729,1152]{2,1,0:T(8,128)(2,1)} collective-permute-done((bf16[1,729,1152]{2,1,0:T(8,128)(2,1)}, bf16[1,729,1152]{2,1,0:T(8,128)(2,1)}, u32[]{:S(2)}, u32[]{:S(2)}) %collective-permute-start) | collective-permute-done | bytes 1679648 | tf_op jit(solution)/shard_map/while/body/eval_jaxpr/ppermute | solution.py:15
  826.4 130.8 %all-reduce.5.cloned.1.call-done = f32[729,1152]{1,0:T(8,128)} async-done(((f32[729,1152]{1,0:T(8,128)}), f32[729,1152]{1,0:T(8,128)}) %all-reduce.5.cloned.1.call-update) | async-done | bytes 3359248 | tf_op jit(solution)/shard_map/while/body/eval_jaxpr/psum | solution.py:86
  957.2 4.7 bitcast_dynamic-update-slice_fusion.17
  978.4 124.3 %all-reduce.7.cloned.1.call-done = f32[729,1152]{1,0:T(8,128)} async-done(((f32[729,1152]{1,0:T(8,128)}), f32[729,1152]{1,0:T(8,128)}) %all-reduce.7.cloned.1.call-update) | async-done | bytes 3359248 | tf_op jit(solution)/shard_map/while/body/eval_jaxpr/psum | solution.py:93
  1116.8 29.8 %collective-permute-done = bf16[1,729,1152]{2,1,0:T(8,128)(2,1)} collective-permute-done((bf16[1,729,1152]{2,1,0:T(8,128)(2,1)}, bf16[1,729,1152]{2,1,0:T(8,128)(2,1)}, u32[]{:S(2)}, u32[]{:S(2)}) %collective-permute-start) | collective-permute-done | bytes 1679648 | tf_op jit(solution)/shard_map/while/body/eval_jaxpr/ppermute | solution.py:15
  1149.6 1438.0 %while.67 = (s32[]{:T(128)}, f32[729,1152]{1,0:T(8,128)S(1)}, f32[3,1152,288]{1,2,0:T(8,128)}, f32[288,1152]{1,0:T(8,128)}, f32[1152,1076]{0,1:T(8,128)}, /*inde...) while((s32[]{:T(128)}, f32[729,1152]{1,0:T(8,128)S(1)}, ...), condition=%wide.region_31.32_spmd.clone, body=%wide.region_10.31_spmd.clone.sunk | while | flops 12742931456 | bytes 524523008 | solution.py:279
  1175.7 6.1 convert_reduce_fusion.16
  1183.1 4.6 convolution_bitcast_fusion.7
  1197.0 5.4 fusion.210
  1202.4 219.8 %all-gather.22.cloned.1.call-done = f32[4,729,1152]{2,1,0:T(8,128)} async-done(((f32[1,729,1152]{2,1,0:T(8,128)}), f32[4,729,1152]{2,1,0:T(8,128)}) %all-gather.22.cloned.1.call-update) | async-done | bytes 13436944 | tf_op jit(solution)/shard_map/while/body/eval_jaxpr/all_gather | solution.py:138
  1422.2 6.7 fusion.209
  1438.7 4.6 multiply_reduce_fusion.17
  1443.3 10.2 multiply_convert_fusion.2
  1458.9 5.5 convert_reduce_fusion.18
  1474.1 6.3 fusion.215
  1480.4 5.2 fusion.216
  1490.9 104.8 %all-reduce.9.cloned.1.call-done = f32[729,1152]{1,0:T(8,128)} async-done(((f32[729,1152]{1,0:T(8,128)}), f32[729,1152]{1,0:T(8,128)}) %all-reduce.9.cloned.1.call-update) | async-done | bytes 3359248 | tf_op jit(solution)/shard_map/while/body/eval_jaxpr/psum | solution.py:196
  1609.3 34.7 %collective-permute-done.1 = bf16[1,729,1152]{2,1,0:T(8,128)(2,1)S(1)} collective-permute-done((bf16[1,729,1152]{2,1,0:T(8,128)(2,1)S(1)}, bf16[1,729,1152]{2,1,0:T(8,128)(2,1)S(1)}, u32[]{:S(2)}, u32[]{:S(2)}) %collective-permute-start.1) | collective-permute-done | bytes 1679648 | tf_op jit(solution)/shard_map/while/body/eval_jaxpr/ppermute | solution.py:15
  1647.9 6.1 convert_reduce_fusion.16
  1669.4 5.3 fusion.210
  1674.7 217.7 %all-gather.22.cloned.1.call-done = f32[4,729,1152]{2,1,0:T(8,128)} async-done(((f32[1,729,1152]{2,1,0:T(8,128)}), f32[4,729,1152]{2,1,0:T(8,128)}) %all-gather.22.cloned.1.call-update) | async-done | bytes 13436944 | tf_op jit(solution)/shard_map/while/body/eval_jaxpr/all_gather | solution.py:138
  1892.4 6.7 fusion.209
  1909.0 4.6 multiply_reduce_fusion.17
  1913.6 10.2 multiply_convert_fusion.2
  1929.2 5.5 convert_reduce_fusion.18
  1944.4 7.7 fusion.215
  1952.1 5.2 fusion.216
  1963.1 102.9 %all-reduce.9.cloned.1.call-done = f32[729,1152]{1,0:T(8,128)} async-done(((f32[729,1152]{1,0:T(8,128)}), f32[729,1152]{1,0:T(8,128)}) %all-reduce.9.cloned.1.call-update) | async-done | bytes 3359248 | tf_op jit(solution)/shard_map/while/body/eval_jaxpr/psum | solution.py:196
  2079.6 34.7 %collective-permute-done.1 = bf16[1,729,1152]{2,1,0:T(8,128)(2,1)S(1)} collective-permute-done((bf16[1,729,1152]{2,1,0:T(8,128)(2,1)S(1)}, bf16[1,729,1152]{2,1,0:T(8,128)(2,1)S(1)}, u32[]{:S(2)}, u32[]{:S(2)}) %collective-permute-start.1) | collective-permute-done | bytes 1679648 | tf_op jit(solution)/shard_map/while/body/eval_jaxpr/ppermute | solution.py:15
  2118.2 6.1 convert_reduce_fusion.16
  2125.5 4.6 convolution_bitcast_fusion.7
  2139.7 5.3 fusion.210
  2145.0 217.7 %all-gather.22.cloned.1.call-done = f32[4,729,1152]{2,1,0:T(8,128)} async-done(((f32[1,729,1152]{2,1,0:T(8,128)}), f32[4,729,1152]{2,1,0:T(8,128)}) %all-gather.22.cloned.1.call-update) | async-done | bytes 13436944 | tf_op jit(solution)/shard_map/while/body/eval_jaxpr/all_gather | solution.py:138
  2362.7 6.7 fusion.209
  2379.2 4.6 multiply_reduce_fusion.17
  2383.8 10.2 multiply_convert_fusion.2
  2399.4 5.5 convert_reduce_fusion.18
  2414.6 7.7 fusion.215
  2422.4 5.2 fusion.216
  2433.3 102.9 %all-reduce.9.cloned.1.call-done = f32[729,1152]{1,0:T(8,128)} async-done(((f32[729,1152]{1,0:T(8,128)}), f32[729,1152]{1,0:T(8,128)}) %all-reduce.9.cloned.1.call-update) | async-done | bytes 3359248 | tf_op jit(solution)/shard_map/while/body/eval_jaxpr/psum | solution.py:196
  2549.9 34.7 %collective-permute-done.1 = bf16[1,729,1152]{2,1,0:T(8,128)(2,1)S(1)} collective-permute-done((bf16[1,729,1152]{2,1,0:T(8,128)(2,1)S(1)}, bf16[1,729,1152]{2,1,0:T(8,128)(2,1)S(1)}, u32[]{:S(2)}, u32[]{:S(2)}) %collective-permute-start.1) | collective-permute-done | bytes 1679648 | tf_op jit(solution)/shard_map/while/body/eval_jaxpr/ppermute | solution.py:15
  2595.9 6.0 copy.137
  2619.0 6.0 copy.129
  2625.0 5.2 constant_dynamic-slice_fusion.3
  2630.2 31.6 %rev.4 = bf16[2,1,729,1152]{3,0,2,1:T(2,128)(2,1)} reverse(bf16[2,1,729,1152]{3,0,2,1:T(2,128)(2,1)} %constant_dynamic-slice_fusion.3), dimensions={0} | reverse | bytes 6718464 | tf_op jit(solution)/shard_map/jit(_flip)/rev | solution.py:303
  2668.4 6.6 all-reduce
  2680.1 13.0 reduce-scatter.19.cloned.1.call-done
  2698.2 32.0 %reduce-scatter.23.cloned.1.call-done = bf16[288,1076]{1,0:T(8,128)(2,1)} async-done(((bf16[1152,1076]{1,0:T(8,128)(2,1)}), bf16[288,1076]{1,0:T(8,128)(2,1)}) %reduce-scatter.23.cloned.1.call-update) | async-done | bytes 619792
  2733.4 34.1 %reduce-scatter.25.cloned.1.call-done = bf16[288,1076]{1,0:T(8,128)(2,1)} async-done(((bf16[1152,1076]{1,0:T(8,128)(2,1)}), bf16[288,1076]{1,0:T(8,128)(2,1)}) %reduce-scatter.25.cloned.1.call-update) | async-done | bytes 619792
  (755 shorter events, 402.7 us)
Async XLA Ops:
  7.2 58.4 %all-gather.16.cloned.1.call-start = ((), (), s32[]{:S(2)}) async-start(), calls=%async_computation.6 | async-start | bytes 4423680 | tf_op jit(solution)/shard_map/all_gather | solution.py:228
  9.8 25.6 copy-start.64
  9.8 68.9 %all-gather.20.cloned.1.call-start = ((), (), s32[]{:S(2)}) async-start(), calls=%async_computation.8 | async-start | bytes 3317760 | tf_op jit(solution)/shard_map/all_gather | solution.py:231
  10.5 95.4 %all-gather.18.cloned.1.call-start = ((), (), s32[]{:S(2)}) async-start(), calls=%async_computation.7 | async-start | bytes 3317760 | tf_op jit(solution)/shard_map/all_gather | solution.py:230
  125.5 150.8 %all-reduce.5.cloned.1.call-start = ((), (), s32[]{:S(2)}) async-start(), calls=%async_computation.15 | async-start | bytes 6782976 | tf_op jit(solution)/shard_map/while/body/eval_jaxpr/psum | solution.py:86
  142.6 133.7 %copy-start.41 = (f32[1152]{0:T(1024)S(1)}, f32[1152]{0:T(1024)}, u32[]{:S(2)}) copy-start(f32[1152]{0:T(1024)} %get-tuple-element.1534) | copy-start | bytes 13828 | tf_op jit(solution)/shard_map/while
  145.5 276.3 %all-reduce.7.cloned.1.call-start = ((), (), s32[]{:S(2)}) async-start(), calls=%async_computation.16 | async-start | bytes 6782976 | tf_op jit(solution)/shard_map/while/body/eval_jaxpr/psum | solution.py:93
  293.4 128.4 %copy-start.42 = (f32[1152]{0:T(1024)S(1)}, f32[1152]{0:T(1024)}, u32[]{:S(2)}) copy-start(f32[1152]{0:T(1024)} %get-tuple-element.1533) | copy-start | bytes 13828 | tf_op jit(solution)/shard_map/while
  421.8 8.8 copy-start.20
  426.0 39.8 %collective-permute-start = (bf16[1,729,1152]{2,1,0:T(8,128)(2,1)}, bf16[1,729,1152]{2,1,0:T(8,128)(2,1)}, u32[]{:S(2)}, u32[]{:S(2)}) collective-permute-start(bf16[1,729,1152]{2,1,0:T(8,128)(2,1)} %bitcast.322), channel_id=1, source_target_pairs={{0,16},{1,17},{2,18},{3,19},{4,20},{5,21},{6,22},{7,23},{8,24},{9,... | collective-permute-start | bytes 5038856 | tf_op jit(solution)/shard_map/while/body/eval_jaxpr/ppermute | solution.py:15
  433.8 32.0 %copy-start.28 = (bf16[2,1,729,1152]{3,2,1,0:T(8,128)(2,1)S(1)}, bf16[2,1,729,1152]{3,2,1,0:T(8,128)(2,1)}, u32[]{:S(2)}) copy-start(bf16[2,1,729,1152]{3,2,1,0:T(8,128)(2,1)} %copy-done.27) | copy-start | bytes 10077700 | tf_op jit(solution)/shard_map/while
  433.8 32.0 %copy-start.45 = (bf16[2,1152]{1,0:T(2,128)(2,1)S(1)}, bf16[2,1152]{1,0:T(2,128)(2,1)}, u32[]{:S(2)}) copy-start(bf16[2,1152]{1,0:T(2,128)(2,1)} %copy-done.44) | copy-start | bytes 13828 | tf_op jit(solution)/shard_map/while
  433.8 32.0 %copy-start.50 = (bf16[4,1152]{1,0:T(4,128)(2,1)S(1)}, bf16[4,1152]{1,0:T(4,128)(2,1)}, u32[]{:S(2)}) copy-start(bf16[4,1152]{1,0:T(4,128)(2,1)} %copy-done.49) | copy-start | bytes 27652 | tf_op jit(solution)/shard_map/while
  433.8 32.0 %copy-start.60 = (bf16[1,2,288]{2,1,0:T(2,128)(2,1)S(1)}, bf16[1,2,288]{2,1,0:T(2,128)(2,1)}, u32[]{:S(2)}) copy-start(bf16[1,2,288]{2,1,0:T(2,128)(2,1)} %get-tuple-element.1902) | copy-start | bytes 3460 | tf_op jit(solution)/shard_map/while
  433.8 32.0 %copy-start.68 = (s32[3]{0:T(128)S(1)}, s32[3]{0:T(128)}, u32[]{:S(2)}) copy-start(s32[3]{0:T(128)} %copy-done.67) | copy-start | bytes 40 | tf_op jit(solution)/shard_map/while
  465.9 150.8 %all-reduce.5.cloned.1.call-start = ((), (), s32[]{:S(2)}) async-start(), calls=%async_computation.15 | async-start | bytes 6782976 | tf_op jit(solution)/shard_map/while/body/eval_jaxpr/psum | solution.py:86
  483.0 133.7 %copy-start.41 = (f32[1152]{0:T(1024)S(1)}, f32[1152]{0:T(1024)}, u32[]{:S(2)}) copy-start(f32[1152]{0:T(1024)} %get-tuple-element.1534) | copy-start | bytes 13828 | tf_op jit(solution)/shard_map/while
  485.9 276.4 %all-reduce.7.cloned.1.call-start = ((), (), s32[]{:S(2)}) async-start(), calls=%async_computation.16 | async-start | bytes 6782976 | tf_op jit(solution)/shard_map/while/body/eval_jaxpr/psum | solution.py:93
  634.0 128.4 %copy-start.42 = (f32[1152]{0:T(1024)S(1)}, f32[1152]{0:T(1024)}, u32[]{:S(2)}) copy-start(f32[1152]{0:T(1024)} %get-tuple-element.1533) | copy-start | bytes 13828 | tf_op jit(solution)/shard_map/while
  762.3 8.7 copy-start.20
  766.5 39.8 %collective-permute-start = (bf16[1,729,1152]{2,1,0:T(8,128)(2,1)}, bf16[1,729,1152]{2,1,0:T(8,128)(2,1)}, u32[]{:S(2)}, u32[]{:S(2)}) collective-permute-start(bf16[1,729,1152]{2,1,0:T(8,128)(2,1)} %bitcast.322), channel_id=1, source_target_pairs={{0,16},{1,17},{2,18},{3,19},{4,20},{5,21},{6,22},{7,23},{8,24},{9,... | collective-permute-start | bytes 5038856 | tf_op jit(solution)/shard_map/while/body/eval_jaxpr/ppermute | solution.py:15
  774.3 32.0 %copy-start.28 = (bf16[2,1,729,1152]{3,2,1,0:T(8,128)(2,1)S(1)}, bf16[2,1,729,1152]{3,2,1,0:T(8,128)(2,1)}, u32[]{:S(2)}) copy-start(bf16[2,1,729,1152]{3,2,1,0:T(8,128)(2,1)} %copy-done.27) | copy-start | bytes 10077700 | tf_op jit(solution)/shard_map/while
  774.3 32.0 %copy-start.45 = (bf16[2,1152]{1,0:T(2,128)(2,1)S(1)}, bf16[2,1152]{1,0:T(2,128)(2,1)}, u32[]{:S(2)}) copy-start(bf16[2,1152]{1,0:T(2,128)(2,1)} %copy-done.44) | copy-start | bytes 13828 | tf_op jit(solution)/shard_map/while
  774.3 32.0 %copy-start.50 = (bf16[4,1152]{1,0:T(4,128)(2,1)S(1)}, bf16[4,1152]{1,0:T(4,128)(2,1)}, u32[]{:S(2)}) copy-start(bf16[4,1152]{1,0:T(4,128)(2,1)} %copy-done.49) | copy-start | bytes 27652 | tf_op jit(solution)/shard_map/while
  774.3 32.0 %copy-start.60 = (bf16[1,2,288]{2,1,0:T(2,128)(2,1)S(1)}, bf16[1,2,288]{2,1,0:T(2,128)(2,1)}, u32[]{:S(2)}) copy-start(bf16[1,2,288]{2,1,0:T(2,128)(2,1)} %get-tuple-element.1902) | copy-start | bytes 3460 | tf_op jit(solution)/shard_map/while
  774.3 32.0 %copy-start.68 = (s32[3]{0:T(128)S(1)}, s32[3]{0:T(128)}, u32[]{:S(2)}) copy-start(s32[3]{0:T(128)} %copy-done.67) | copy-start | bytes 40 | tf_op jit(solution)/shard_map/while
  806.4 150.8 %all-reduce.5.cloned.1.call-start = ((), (), s32[]{:S(2)}) async-start(), calls=%async_computation.15 | async-start | bytes 6782976 | tf_op jit(solution)/shard_map/while/body/eval_jaxpr/psum | solution.py:86
  823.4 133.7 %copy-start.41 = (f32[1152]{0:T(1024)S(1)}, f32[1152]{0:T(1024)}, u32[]{:S(2)}) copy-start(f32[1152]{0:T(1024)} %get-tuple-element.1534) | copy-start | bytes 13828 | tf_op jit(solution)/shard_map/while
  826.3 276.3 %all-reduce.7.cloned.1.call-start = ((), (), s32[]{:S(2)}) async-start(), calls=%async_computation.16 | async-start | bytes 6782976 | tf_op jit(solution)/shard_map/while/body/eval_jaxpr/psum | solution.py:93
  974.3 128.4 %copy-start.42 = (f32[1152]{0:T(1024)S(1)}, f32[1152]{0:T(1024)}, u32[]{:S(2)}) copy-start(f32[1152]{0:T(1024)} %get-tuple-element.1533) | copy-start | bytes 13828 | tf_op jit(solution)/shard_map/while
  1102.7 8.7 copy-start.20
  1106.8 39.8 %collective-permute-start = (bf16[1,729,1152]{2,1,0:T(8,128)(2,1)}, bf16[1,729,1152]{2,1,0:T(8,128)(2,1)}, u32[]{:S(2)}, u32[]{:S(2)}) collective-permute-start(bf16[1,729,1152]{2,1,0:T(8,128)(2,1)} %bitcast.322), channel_id=1, source_target_pairs={{0,16},{1,17},{2,18},{3,19},{4,20},{5,21},{6,22},{7,23},{8,24},{9,... | collective-permute-start | bytes 5038856 | tf_op jit(solution)/shard_map/while/body/eval_jaxpr/ppermute | solution.py:15
  1114.6 32.0 %copy-start.28 = (bf16[2,1,729,1152]{3,2,1,0:T(8,128)(2,1)S(1)}, bf16[2,1,729,1152]{3,2,1,0:T(8,128)(2,1)}, u32[]{:S(2)}) copy-start(bf16[2,1,729,1152]{3,2,1,0:T(8,128)(2,1)} %copy-done.27) | copy-start | bytes 10077700 | tf_op jit(solution)/shard_map/while
  1114.6 32.0 %copy-start.45 = (bf16[2,1152]{1,0:T(2,128)(2,1)S(1)}, bf16[2,1152]{1,0:T(2,128)(2,1)}, u32[]{:S(2)}) copy-start(bf16[2,1152]{1,0:T(2,128)(2,1)} %copy-done.44) | copy-start | bytes 13828 | tf_op jit(solution)/shard_map/while
  1114.6 32.0 %copy-start.50 = (bf16[4,1152]{1,0:T(4,128)(2,1)S(1)}, bf16[4,1152]{1,0:T(4,128)(2,1)}, u32[]{:S(2)}) copy-start(bf16[4,1152]{1,0:T(4,128)(2,1)} %copy-done.49) | copy-start | bytes 27652 | tf_op jit(solution)/shard_map/while
  1114.6 32.0 %copy-start.60 = (bf16[1,2,288]{2,1,0:T(2,128)(2,1)S(1)}, bf16[1,2,288]{2,1,0:T(2,128)(2,1)}, u32[]{:S(2)}) copy-start(bf16[1,2,288]{2,1,0:T(2,128)(2,1)} %get-tuple-element.1902) | copy-start | bytes 3460 | tf_op jit(solution)/shard_map/while
  1114.6 32.0 %copy-start.68 = (s32[3]{0:T(128)S(1)}, s32[3]{0:T(128)}, u32[]{:S(2)}) copy-start(s32[3]{0:T(128)} %copy-done.67) | copy-start | bytes 40 | tf_op jit(solution)/shard_map/while
  1172.1 250.1 %all-gather.22.cloned.1.call-start = ((), (), s32[]{:S(2)}) async-start(), calls=%async_computation.17 | async-start | bytes 16957440 | tf_op jit(solution)/shard_map/while/body/eval_jaxpr/all_gather | solution.py:138
  1175.7 7.3 copy-start.66
  1187.7 408.0 %all-reduce.9.cloned.1.call-start = ((), (), s32[]{:S(2)}) async-start(), calls=%async_computation.18 | async-start | bytes 6782976 | tf_op jit(solution)/shard_map/while/body/eval_jaxpr/psum | solution.py:196
  1469.1 11.2 slice-start.3
  1603.5 40.5 %collective-permute-start.1 = (bf16[1,729,1152]{2,1,0:T(8,128)(2,1)S(1)}, bf16[1,729,1152]{2,1,0:T(8,128)(2,1)S(1)}, u32[]{:S(2)}, u32[]{:S(2)}) collective-permute-start(bf16[1,729,1152]{2,1,0:T(8,128)(2,1)S(1)} %bitcast.386), channel_id=1, source_target_pairs={{16,0},{17,1},{18,2},{19,3},{20,4},{21,5},{22,6},{23,7},{24,8},{25... | collective-permute-start | bytes 5038856 | tf_op jit(solution)/shard_map/while/body/eval_jaxpr/ppermute | solution.py:15
  1609.2 35.0 %copy-start.32 = (f32[3,1152,288]{1,2,0:T(8,128)}, f32[3,1152,288]{1,2,0:T(8,128)S(1)}, u32[]{:S(2)}) copy-start(f32[3,1152,288]{1,2,0:T(8,128)S(1)} %bitcast_add_fusion.2) | copy-start | bytes 11943940 | tf_op jit(solution)/shard_map/while
  1644.3 248.2 %all-gather.22.cloned.1.call-start = ((), (), s32[]{:S(2)}) async-start(), calls=%async_computation.17 | async-start | bytes 16957440 | tf_op jit(solution)/shard_map/while/body/eval_jaxpr/all_gather | solution.py:138
  1659.9 406.1 %all-reduce.9.cloned.1.call-start = ((), (), s32[]{:S(2)}) async-start(), calls=%async_computation.18 | async-start | bytes 6782976 | tf_op jit(solution)/shard_map/while/body/eval_jaxpr/psum | solution.py:196
  1939.4 12.7 slice-start.3
  1944.3 7.8 copy-start.26
  1944.3 7.8 slice-start.4
  2073.8 40.5 %collective-permute-start.1 = (bf16[1,729,1152]{2,1,0:T(8,128)(2,1)S(1)}, bf16[1,729,1152]{2,1,0:T(8,128)(2,1)S(1)}, u32[]{:S(2)}, u32[]{:S(2)}) collective-permute-start(bf16[1,729,1152]{2,1,0:T(8,128)(2,1)S(1)} %bitcast.386), channel_id=1, source_target_pairs={{16,0},{17,1},{18,2},{19,3},{20,4},{21,5},{22,6},{23,7},{24,8},{25... | collective-permute-start | bytes 5038856 | tf_op jit(solution)/shard_map/while/body/eval_jaxpr/ppermute | solution.py:15
  2079.5 35.0 %copy-start.32 = (f32[3,1152,288]{1,2,0:T(8,128)}, f32[3,1152,288]{1,2,0:T(8,128)S(1)}, u32[]{:S(2)}) copy-start(f32[3,1152,288]{1,2,0:T(8,128)S(1)} %bitcast_add_fusion.2) | copy-start | bytes 11943940 | tf_op jit(solution)/shard_map/while
  2114.5 248.2 %all-gather.22.cloned.1.call-start = ((), (), s32[]{:S(2)}) async-start(), calls=%async_computation.17 | async-start | bytes 16957440 | tf_op jit(solution)/shard_map/while/body/eval_jaxpr/all_gather | solution.py:138
  2118.2 7.3 copy-start.66
  2130.2 406.1 %all-reduce.9.cloned.1.call-start = ((), (), s32[]{:S(2)}) async-start(), calls=%async_computation.18 | async-start | bytes 6782976 | tf_op jit(solution)/shard_map/while/body/eval_jaxpr/psum | solution.py:196
  2409.6 12.7 slice-start.3
  2414.6 7.8 copy-start.26
  2414.6 7.8 slice-start.4
  2544.0 40.5 %collective-permute-start.1 = (bf16[1,729,1152]{2,1,0:T(8,128)(2,1)S(1)}, bf16[1,729,1152]{2,1,0:T(8,128)(2,1)S(1)}, u32[]{:S(2)}, u32[]{:S(2)}) collective-permute-start(bf16[1,729,1152]{2,1,0:T(8,128)(2,1)S(1)} %bitcast.386), channel_id=1, source_target_pairs={{16,0},{17,1},{18,2},{19,3},{20,4},{21,5},{22,6},{23,7},{24,8},{25... | collective-permute-start | bytes 5038856 | tf_op jit(solution)/shard_map/while/body/eval_jaxpr/ppermute | solution.py:15
  2549.7 35.0 %copy-start.32 = (f32[3,1152,288]{1,2,0:T(8,128)}, f32[3,1152,288]{1,2,0:T(8,128)S(1)}, u32[]{:S(2)}) copy-start(f32[3,1152,288]{1,2,0:T(8,128)S(1)} %bitcast_add_fusion.2) | copy-start | bytes 11943940 | tf_op jit(solution)/shard_map/while
  2587.6 87.4 %reduce-scatter.27.cloned.1.call-start = ((), (), s32[]{:S(2)}) async-start(), calls=%async_computation.13 | async-start | bytes 368640
  2588.6 88.0 %reduce-scatter.29.cloned.1.call-start = ((), (), s32[]{:S(2)}) async-start(), calls=%async_computation.14 | async-start | bytes 368640
  2589.6 88.6 %reduce-scatter.21.cloned.1.call-start = ((), (), s32[]{:S(2)}) async-start(), calls=%async_computation.10 | async-start | bytes 1105920
  2592.3 100.9 %reduce-scatter.19.cloned.1.call-start = ((), (), s32[]{:S(2)}) async-start(), calls=%async_computation.9 | async-start | bytes 2580480
  2606.1 124.1 %reduce-scatter.23.cloned.1.call-start = ((), (), s32[]{:S(2)}) async-start(), calls=%async_computation.11 | async-start | bytes 3317760
  2612.2 155.4 %reduce-scatter.25.cloned.1.call-start = ((), (), s32[]{:S(2)}) async-start(), calls=%async_computation.12 | async-start | bytes 3317760
  (167 other events, 558.5 us)
Sparse Core Ops, SparseCore 0:
  10.1 40.3 all-gather.15
  52.1 26.5 all-gather.19
  80.2 25.7 all-gather.17
  145.6 130.6 all-reduce.4
  293.6 128.1 all-reduce.6
  486.0 130.6 all-reduce.4
  634.1 128.1 all-reduce.6
  826.5 130.6 all-reduce.4
  974.5 128.1 all-reduce.6
  1187.8 234.2 all-gather.21
  1469.2 126.4 all-reduce.8
  1660.0 232.3 all-gather.21
  1939.5 126.4 all-reduce.8
  2130.3 232.3 all-gather.21
  2409.7 126.4 all-reduce.8
  2591.1 18.3 reduce-scatter.26
  2612.4 20.2 reduce-scatter.28
  2635.7 23.7 reduce-scatter.20
  2662.1 30.9 reduce-scatter.18
  2695.5 34.7 reduce-scatter.22
  2732.8 34.7 reduce-scatter.24
